TPU v7x, 512 devices: a whole 4x8x8 slice. The times are simulated.
512 devices in a mesh: shard: 128 (over y, z, core), tensor: 4 (over x).
Axes of the slice: x: 4, y: 8, z: 8, core: 2. Of those that a mesh axis runs over, the one named last changes fastest.
Arguments:
- grad_query: bfloat16 [128, 1024, 512], P('shard', None, 'tensor'), may hold values from -8 to 8
- error_query: float32 [128, 1024, 512], P('shard', None, 'tensor'), may hold values from -3 to 3
- grad_output: bfloat16 [128, 512, 1024], P('shard', 'tensor'), may hold values from -8 to 8
- error_output: float32 [128, 512, 1024], P('shard', 'tensor'), may hold values from -3 to 3
- start_query: float32 [512, 32], P('tensor'), may hold values from -6 to 6
- start_output: float32 [1024, 32], replicated, may hold values from -6 to 6
- weight_query: float32 [1024, 512], P('shard', 'tensor'), may hold values from -0.1875 to 0.1875
- weight_output: float32 [512, 1024], P('tensor', 'shard'), may hold values from -0.25 to 0.25
- moment_query: float32 [1024, 512], P('shard', 'tensor'), may hold values from -1.2 to 1.2
- moment_output: float32 [512, 1024], P('tensor', 'shard'), may hold values from -1.2 to 1.2
- grad_vector: bfloat16 [128, 3584], P('shard'), may hold values from -12 to 12
- moment_vector: float32 [3584], P('shard'), may hold values from -1.2 to 1.2
- weight_vector: float32 [3584], P('shard'), may hold values from 0.5 to 1.5
Outputs:
- new_error_query: float32 [128, 1024, 512], P('shard', None, 'tensor')
- new_error_output: float32 [128, 512, 1024], P('shard', 'tensor')
- new_moment_query: float32 [1024, 512], P('shard', 'tensor')
- new_moment_output: float32 [512, 1024], P('tensor', 'shard')
- new_weight_query: float32 [1024, 512], P(None, 'tensor')
- new_weight_output: float32 [512, 1024], P('tensor')
- new_moment_vector: float32 [3584], P('shard')
- new_weight_vector: float32 [3584], replicated
All inputs are finite; a program needn't handle non-finite values.
Results may differ from a plain program's by a relative error of at most 0.0003.
Values sent between devices are 32-bit elements; how exact they have to be, the bound alone decides.
No kernel may reach another device: no remote copies, remote signals or barrier semaphores. Data moves between devices by JAX's collectives and lax.ppermute only.
A program may use at most 64 MiB of HBM per device.

v0:
```python
import jax
import jax.numpy as jnp
from jax import lax
from jax.sharding import PartitionSpec as P

ROUNDS = 2
highest = lax.Precision.HIGHEST


def product(left, right):
    return jnp.dot(left, right, precision=highest, preferred_element_type=jnp.float32)


def product_inner(left, right):
    return lax.dot_general(
        left, right, (((0,), (0,)), ((), ())), precision=highest, preferred_element_type=jnp.float32
    )


def solve_rows(gram, factor):
    lower = jnp.linalg.cholesky(gram)
    return jax.scipy.linalg.solve_triangular(lower, factor.T, lower=True).T


def orthonormal(factor):
    return solve_rows(product_inner(factor, factor), factor)


def orthonormal_rows(factor):
    gram = lax.psum(product_inner(factor, factor), "tensor")
    return solve_rows(gram, factor)


def local(
    grad_query,
    error_query,
    grad_output,
    error_output,
    start_query,
    start_output,
    weight_query,
    weight_output,
    moment_query,
    moment_output,
    grad_vector,
    moment_vector,
    weight_vector,
):
    replicas = lax.axis_size("shard")
    shard_index = lax.axis_index("shard")
    total_query = grad_query[0].astype(jnp.float32) + error_query[0]
    total_output = grad_output[0].astype(jnp.float32) + error_output[0]
    factor_query = start_query
    factor_output = start_output
    for turn in range(ROUNDS):
        part_query = product(total_query, factor_query)
        part_output = product(total_output, factor_output)
        sum_query = lax.psum(part_query, ("shard", "tensor"))
        sum_output = lax.psum(part_output, "shard")
        left_query = orthonormal(sum_query)
        left_output = orthonormal_rows(sum_output)
        right_query_part = product_inner(total_query, left_query)
        right_output_part = product_inner(total_output, left_output)
        factor_query = lax.psum(right_query_part, "shard")
        factor_output = lax.psum(right_output_part, ("shard", "tensor"))
    approx_query = product(left_query, factor_query.T) / replicas
    approx_output = product(left_output, factor_output.T) / replicas
    new_error_query = (total_query - approx_query)[None]
    new_error_output = (total_output - approx_output)[None]
    rows_block = moment_query.shape[0]
    block_query = lax.dynamic_slice_in_dim(approx_query, shard_index * rows_block, rows_block, 0)
    cols_block = moment_output.shape[1]
    block_output = lax.dynamic_slice_in_dim(approx_output, shard_index * cols_block, cols_block, 1)
    new_moment_query = 0.9 * moment_query + block_query
    new_moment_output = 0.9 * moment_output + block_output
    stepped_query = weight_query - 0.01 * new_moment_query
    stepped_output = weight_output - 0.01 * new_moment_output
    local_vector = grad_vector[0].astype(jnp.float32)
    vector_block = moment_vector.shape[0]
    vector_whole = lax.psum(local_vector, "shard")
    vector_part = lax.dynamic_slice_in_dim(
        vector_whole, shard_index * vector_block, vector_block, 0
    )
    vector_mean = vector_part / replicas
    new_moment_vector = 0.9 * moment_vector + vector_mean
    stepped_vector = weight_vector - 0.01 * new_moment_vector
    new_weight_query, new_weight_output, new_weight_vector = (
        lax.all_gather(stepped_query, "shard", axis=0, tiled=True),
        lax.all_gather(stepped_output, "shard", axis=1, tiled=True),
        lax.all_gather(stepped_vector, "shard", axis=0, tiled=True),
    )
    return (
        new_error_query,
        new_error_output,
        new_moment_query,
        new_moment_output,
        new_weight_query,
        new_weight_output,
        new_moment_vector,
        new_weight_vector,
    )


def solution(mesh):
    in_specs = (
        P("shard", None, "tensor"),
        P("shard", None, "tensor"),
        P("shard", "tensor", None),
        P("shard", "tensor", None),
        P("tensor", None),
        P(),
        P("shard", "tensor"),
        P("tensor", "shard"),
        P("shard", "tensor"),
        P("tensor", "shard"),
        P("shard", None),
        P("shard"),
        P("shard"),
    )
    out_specs = (
        P("shard", None, "tensor"),
        P("shard", "tensor", None),
        P("shard", "tensor"),
        P("tensor", "shard"),
        P(None, "tensor"),
        P("tensor", None),
        P("shard"),
        P(),
    )
    return jax.shard_map(local, mesh=mesh, in_specs=in_specs, out_specs=out_specs, check_vma=False)
```

profile of v0, /device:TPU:1, one launch (start us, length us, event | category | flops | bytes accessed | tf_op | source)
XLA Modules:
  0.0 2203.4 jit_solution(7634404734054702130)
XLA Ops:
  7.2 0.0 all-reduce.10.cloned.1.call-start
  7.2 1.2 copy.45
  8.4 0.2 copy.46
  8.6 0.4 fusion.6
  9.1 498.1 %psum.81 = f32[128,32]{0,1:T(8,128)S(1)} all-reduce(f32[128,32]{0,1:T(8,128)S(1)} %fusion.6), channel_id=1, replica_groups=mesh['shard'=128,'tensor'=4] {'shard'}, use_global_device_ids=true, to_apply=%region_6.9 | all-reduce | flops 4096 | bytes 32768 | tf_op jit(solution)/shard_map/psum | solution.py:59
  507.2 0.1 fusion.42
  507.3 13.2 psum.82
  520.6 0.1 copy.48
  520.6 2.9 cholesky.96
  523.6 0.6 compare_reduce_fusion.1
  524.2 0.7 fusion.24
  524.9 2.4 custom-call.12
  527.3 0.2 fusion.30
  527.6 1.3 fusion.4
  528.9 1.3 fusion.15
  530.2 0.0 all-reduce.10.cloned.1.call-update
  530.3 0.0 all-reduce.8.cloned.1.call-start
  530.3 1.3 dynamic-slice
  532.3 265.7 %all-reduce.10.cloned.1.call-done = (f32[1024,32]{0,1:T(8,128)}, f32[1024,32]{0,1:T(8,128)}) async-done(((f32[1024,32]{0,1:T(8,128)}, f32[1024,32]{0,1:T(8,128)}), (f32[1024,32]{0,1:T(8,128)}, f32[1024,32]{0,1:T(8,128)})) %all-reduce.10.cloned.1.call-update) | async-done | bytes 262160 | tf_op jit(solution)/shard_map/psum | solution.py:58
  798.0 1.4 fusion.2
  799.4 0.3 fusion.40
  799.7 0.1 copy.43
  799.7 2.9 cholesky.74
  802.7 0.6 compare_reduce_fusion.3
  803.3 0.7 fusion.22
  804.0 2.4 custom-call.10
  806.4 0.3 fusion.20
  806.8 0.4 fusion.13
  807.2 487.8 %all-reduce.4 = (f32[128,32]{0,1:T(8,128)S(1)}, f32[128,32]{0,1:T(8,128)S(1)}, f32[3584]{0:T(1024)S(1)}) all-reduce(f32[128,32]{0,1:T(8,128)S(1)} %fusion.13, f32[128,32]{0,1:T(8,128)S(1)} %fusion.2, f32[3584]{0:T(1024)S(1)} %convert_reduce_fusion), channel_id=1, replica_groups=mesh['shard'=128,'tensor'=4] {'shard'}, use_global_device_ids=true, to_apply=%region_3.6 | all-reduce | flops 11776 | bytes 94208 | tf_op jit(solution)/shard_map/psum | solution.py:64
  1295.0 0.1 fusion.43
  1295.2 12.4 psum.85
  1307.6 0.1 copy.50
  1307.6 2.9 cholesky.107
  1310.6 0.6 compare_reduce_fusion
  1311.2 0.7 fusion.25
  1311.9 2.4 custom-call.13
  1314.3 0.2 fusion.26
  1314.6 1.3 fusion.11
  1315.9 1.3 fusion
  1317.2 0.0 all-reduce.8.cloned.1.call-update
  1317.3 0.6 copy-done.13
  1317.9 0.6 subtract_dynamic-update-slice_fusion
  1318.5 270.5 %all-reduce.8.cloned.1.call-done = (f32[1024,32]{0,1:T(8,128)}, f32[1024,32]{0,1:T(8,128)}) async-done(((f32[1024,32]{0,1:T(8,128)}, f32[1024,32]{0,1:T(8,128)}), (f32[1024,32]{0,1:T(8,128)}, f32[1024,32]{0,1:T(8,128)})) %all-reduce.8.cloned.1.call-update) | async-done | bytes 262160 | tf_op jit(solution)/shard_map/psum | solution.py:58
  1589.0 1.2 fusion.41
  1590.3 0.1 copy.44
  1590.3 2.9 cholesky.85
  1593.3 0.6 compare_reduce_fusion.2
  1593.9 0.7 fusion.23
  1594.6 2.4 custom-call.11
  1597.0 0.3 fusion.18
  1597.4 0.4 fusion.9
  1597.8 487.8 %all-reduce.3 = (f32[128,32]{0,1:T(8,128)S(1)}, f32[3584]{0:T(1024)}) all-reduce(f32[128,32]{0,1:T(8,128)S(1)} %fusion.9, f32[3584]{0:T(1024)S(1)} %get-tuple-element.48), channel_id=1, replica_groups=mesh['shard'=128,'tensor'=4] {'shard'}, use_global_device_ids=true, to_apply=%region_5.8 | all-reduce | flops 7680 | bytes 61440 | tf_op jit(solution)/shard_map/psum | solution.py:64
  2085.6 1.0 convolution_multiply_fusion.1
  2086.6 0.9 fusion.17
  2087.5 0.0 copy-done.6
  2087.5 1.0 convolution_multiply_fusion
  2088.5 0.1 fusion.8
  2088.6 1.0 copy.52
  2089.6 0.6 multiply_subtract_fusion
  2090.2 53.0 %all_gather.10 = f32[128,1024]{0,1:T(8,128)S(1)} all-gather(f32[128,8]{0,1:T(8,128)S(1)} %get-tuple-element.44), channel_id=1, replica_groups=mesh['shard'=128,'tensor'=4] {'shard'}, dimensions={1}, use_global_device_ids=true | all-gather | bytes 528384 | tf_op jit(solution)/shard_map/all_gather | solution.py:89
  2143.3 1.0 copy.53
  2144.3 0.6 multiply_subtract_fusion.1
  2144.9 50.9 %all_gather.9 = f32[1024,128]{1,0:T(8,128)S(1)} all-gather(f32[8,128]{1,0:T(8,128)S(1)} %get-tuple-element.46), channel_id=1, replica_groups=mesh['shard'=128,'tensor'=4] {'shard'}, dimensions={0}, use_global_device_ids=true | all-gather | bytes 528384 | tf_op jit(solution)/shard_map/all_gather | solution.py:88
  2195.8 0.8 copy.63
  (38 shorter events, 0.3 us)
Async XLA Ops:
  7.2 1.5 copy-start
  7.2 1.2 copy-start.5
  7.2 790.8 %all-reduce.10.cloned.1.call-start = ((), (), s32[]{:S(2)}) async-start(), calls=%async_computation.1 | async-start | bytes 524288 | tf_op jit(solution)/shard_map/psum | solution.py:58
  520.6 8.3 copy-start.1
  527.6 1.3 copy-start.2
  527.6 1.3 copy-start.7
  530.3 1058.7 %all-reduce.8.cloned.1.call-start = ((), (), s32[]{:S(2)}) async-start(), calls=%async_computation | async-start | bytes 524288 | tf_op jit(solution)/shard_map/psum | solution.py:58
  530.3 1.9 copy-start.8
  798.0 1.4 copy-start.3
  1317.2 0.7 copy-start.13
  1317.2 0.7 copy-start.14
  1590.2 6.8 copy-start.4
  2086.6 0.9 copy-start.6
  2088.6 1.0 copy-start.9
  2088.6 1.0 copy-start.10
  2143.3 1.0 copy-start.11
  2143.3 1.0 copy-start.12
Sparse Core Ops, SparseCore 0:
  530.4 267.5 all-reduce.9
  1317.3 271.6 all-reduce.7
where the time goes:
time: 2200 us
  blocking collectives  1600 us (73%)
  waiting for transfers between devices  536 us (24%)
  other arithmetic  29.5 us (1%)
    psum x2, blocking collectives, local(): factor_query = lax.psum(right_query_part, 'shard')  976 us
    psum x2, waiting for transfers between devices, local(): sum_query = lax.psum(part_query, ('shard', 'tensor'))  536 us
    psum x1, blocking collectives, local(): sum_output = lax.psum(part_output, 'shard')  498 us
    all_gather x1, blocking collectives, local(): lax.all_gather(stepped_output, 'shard', axis=1, tiled=True)  53 us
    all_gather x1, blocking collectives, local(): lax.all_gather(stepped_query, 'shard', axis=0, tiled=True)  50.9 us
  transfers between devices with their start and end apart: 2, of which 2 were waited for; matrix products, arithmetic and copies ran while one was open for 0% of the time, Pallas kernels for 0%

commit v1 on v0

--- a/solution.py
+++ b/solution.py
@@ -61,7 +61,7 @@
         left_output = orthonormal_rows(sum_output)
         right_query_part = product_inner(total_query, left_query)
         right_output_part = product_inner(total_output, left_output)
-        factor_query = lax.psum(right_query_part, "shard")
+        factor_query = jnp.sum(lax.all_gather(right_query_part, "shard"), axis=0)
         factor_output = lax.psum(right_output_part, ("shard", "tensor"))
     approx_query = product(left_query, factor_query.T) / replicas
     approx_output = product(left_output, factor_output.T) / replicas

time: 2200 us -> 1750 us (0.80)
  blocking collectives: 1600 us -> 1110 us
  waiting for transfers between devices: 536 us -> 563 us
    psum x2 -> x0, blocking collectives: 976 us -> none  [local(): factor_query = lax.psum(right_query_part, 'shard')]
    psum x1 -> x2, blocking collectives: 498 us -> 986 us  [local(): sum_output = lax.psum(part_output, 'shard')]
    all_gather x0 -> x2, waiting for transfers between devices: none -> 23.7 us  [local(): factor_query = jnp.sum(lax.all_gather(right_query_part, 'shard'), axis=0)]
  transfers between devices with their start and end apart: 2 -> 4, of which waited for: 2 -> 3; matrix products, arithmetic and copies ran while one was open for 0% -> 1% of each run, Pallas kernels for 0% -> 0%
where the time goes in v1:
time: 1750 us
  blocking collectives  1110 us (63%)
  waiting for transfers between devices  563 us (32%)
  other arithmetic  30.6 us (2%)
  matrix products  17.7 us (1%)
    psum x2, blocking collectives, local(): sum_output = lax.psum(part_output, 'shard')  986 us
    psum x2, waiting for transfers between devices, local(): sum_query = lax.psum(part_query, ('shard', 'tensor'))  539 us
    all_gather x1, blocking collectives, local(): lax.all_gather(stepped_output, 'shard', axis=1, tiled=True)  49.4 us
    all_gather x1, blocking collectives, local(): lax.all_gather(stepped_query, 'shard', axis=0, tiled=True)  49.2 us
  transfers between devices with their start and end apart: 4, of which 3 were waited for; matrix products, arithmetic and copies ran while one was open for 1% of the time, Pallas kernels for 0%

profile of v1, /device:TPU:1, one launch (start us, length us, event | category | flops | bytes accessed | tf_op | source)
XLA Modules:
  0.0 1747.0 jit_solution(11129014162741478109)
XLA Ops:
  7.3 0.8 convert_reduce_fusion
  8.1 1.1 copy.45
  9.2 1.2 copy.46
  10.5 0.4 fusion.6
  10.9 498.1 %all-reduce.4 = (f32[128,32]{0,1:T(8,128)S(1)}, f32[3584]{0:T(1024)S(1)}) all-reduce(f32[128,32]{0,1:T(8,128)S(1)} %fusion.6, f32[3584]{0:T(1024)S(1)} %convert_reduce_fusion), channel_id=1, replica_groups=mesh['shard'=128,'tensor'=4] {'shard'}, use_global_device_ids=true, to_apply=%region_6.9 | all-reduce | flops 7680 | bytes 61440 | tf_op jit(solution)/shard_map/psum | solution.py:59
  509.0 0.1 fusion.42
  509.2 13.2 psum.66
  522.4 0.1 copy.48
  522.5 2.9 cholesky.96
  525.4 0.6 compare_reduce_fusion.1
  526.1 0.7 fusion.24
  526.7 2.4 custom-call.12
  529.2 0.2 fusion.30
  529.4 1.3 fusion.4
  530.7 1.3 fusion.15
  532.1 0.0 all-gather.5.cloned.1.call-start
  532.1 267.7 %all-reduce.10.cloned.1.call-done = (f32[1024,32]{0,1:T(8,128)}, f32[1024,32]{0,1:T(8,128)}) async-done(((f32[1024,32]{0,1:T(8,128)}, f32[1024,32]{0,1:T(8,128)}), (f32[1024,32]{0,1:T(8,128)}, f32[1024,32]{0,1:T(8,128)})) %all-reduce.10.cloned.1.call-update) | async-done | bytes 262160 | tf_op jit(solution)/shard_map/psum | solution.py:58
  799.8 1.2 fusion.40
  801.1 0.1 copy.43
  801.1 2.9 cholesky.74
  804.1 0.6 compare_reduce_fusion.3
  804.7 0.7 fusion.22
  805.4 2.4 custom-call.10
  807.8 1.2 fusion.20
  809.1 1.1 fusion.13
  810.2 1.3 dynamic-slice
  812.2 0.6 subtract_dynamic-update-slice_fusion
  812.8 1.3 fusion.2
  814.1 487.9 %all-reduce.3 = (f32[128,32]{0,1:T(8,128)S(1)}, f32[3584]{0:T(1024)}) all-reduce(f32[128,32]{0,1:T(8,128)S(1)} %fusion.2, f32[3584]{0:T(1024)S(1)} %get-tuple-element.47), channel_id=1, replica_groups=mesh['shard'=128,'tensor'=4] {'shard'}, use_global_device_ids=true, to_apply=%region_9.0 | all-reduce | flops 7680 | bytes 61440 | tf_op jit(solution)/shard_map/psum | solution.py:59
  1302.1 0.1 fusion.43
  1302.2 12.4 psum.69
  1314.6 0.1 copy.50
  1314.7 2.9 cholesky.107
  1317.6 0.6 compare_reduce_fusion
  1318.3 0.7 fusion.25
  1318.9 2.4 custom-call.13
  1321.4 0.2 fusion.26
  1321.6 1.3 fusion
  1322.9 2.0 copy.57
  1324.9 0.1 bitcast_reduce_fusion.1
  1325.0 1.3 fusion.11
  1326.4 271.5 %all-reduce.8.cloned.1.call-done = (f32[1024,32]{0,1:T(8,128)}, f32[1024,32]{0,1:T(8,128)}) async-done(((f32[1024,32]{0,1:T(8,128)}, f32[1024,32]{0,1:T(8,128)}), (f32[1024,32]{0,1:T(8,128)}, f32[1024,32]{0,1:T(8,128)})) %all-reduce.8.cloned.1.call-update) | async-done | bytes 262160 | tf_op jit(solution)/shard_map/psum | solution.py:58
  1597.9 1.2 fusion.41
  1599.1 0.1 copy.44
  1599.2 2.9 cholesky.85
  1602.1 0.6 compare_reduce_fusion.2
  1602.8 0.7 fusion.23
  1603.4 2.4 custom-call.11
  1605.9 1.2 fusion.18
  1607.2 1.1 fusion.9
  1608.2 1.9 convolution_multiply_fusion
  1610.1 0.1 fusion.8
  1610.2 1.0 copy.52
  1611.2 0.6 multiply_subtract_fusion
  1611.8 49.4 %all_gather.26 = f32[128,1024]{0,1:T(8,128)S(1)} all-gather(f32[128,8]{0,1:T(8,128)S(1)} %get-tuple-element.43), channel_id=1, replica_groups=mesh['shard'=128,'tensor'=4] {'shard'}, dimensions={1}, use_global_device_ids=true | all-gather | bytes 528384 | tf_op jit(solution)/shard_map/all_gather | solution.py:89
  1661.2 1.0 copy.53
  1662.2 23.7 %all-gather.7.cloned.1.call-done = f32[16384,32]{0,1:T(8,128)} async-done(((f32[128,32]{0,1:T(8,128)}), f32[16384,32]{0,1:T(8,128)}) %all-gather.7.cloned.1.call-update) | async-done | bytes 2097168 | tf_op jit(solution)/shard_map/all_gather | solution.py:64
  1685.9 2.0 copy.58
  1687.9 0.1 bitcast_reduce_fusion
  1688.1 1.0 convolution_multiply_fusion.1
  1689.1 0.9 fusion.17
  1689.9 0.6 multiply_subtract_fusion.1
  1690.5 49.2 %all_gather.25 = f32[1024,128]{1,0:T(8,128)S(1)} all-gather(f32[8,128]{1,0:T(8,128)S(1)} %get-tuple-element.45), channel_id=1, replica_groups=mesh['shard'=128,'tensor'=4] {'shard'}, dimensions={0}, use_global_device_ids=true | all-gather | bytes 528384 | tf_op jit(solution)/shard_map/all_gather | solution.py:88
  1739.7 0.8 copy.65
  (37 shorter events, 0.4 us)
Async XLA Ops:
  7.2 3.3 copy-start
  7.2 523.6 %copy-start.1 = (f32[1,1024,128]{2,1,0:T(8,128)S(1)}, f32[1,1024,128]{2,1,0:T(8,128)}, u32[]{:S(2)}) copy-start(f32[1,1024,128]{2,1,0:T(8,128)} %param.19) | copy-start | bytes 1572868
  7.2 523.6 %copy-start.2 = (bf16[1,1024,128]{2,1,0:T(8,128)(2,1)S(1)}, bf16[1,1024,128]{2,1,0:T(8,128)(2,1)}, u32[]{:S(2)}) copy-start(bf16[1,1024,128]{2,1,0:T(8,128)(2,1)} %param.18) | copy-start | bytes 786436
  7.2 523.5 %copy-start.3 = (f32[128,32]{0,1:T(8,128)S(1)}, f32[128,32]{0,1:T(8,128)}, u32[]{:S(2)}) copy-start(f32[128,32]{0,1:T(8,128)} %param.22) | copy-start | bytes 49156
  7.2 792.6 %all-reduce.10.cloned.1.call-start = ((), (), s32[]{:S(2)}) async-start(), calls=%async_computation.3 | async-start | bytes 524288 | tf_op jit(solution)/shard_map/psum | solution.py:58
  10.9 801.2 %copy-start.8 = (f32[28]{0:T(128)S(1)}, f32[28]{0:T(128)}, u32[]{:S(2)}) copy-start(f32[28]{0:T(128)} %param.30) | copy-start | bytes 340
  10.9 801.2 %copy-start.9 = (f32[28]{0:T(128)S(1)}, f32[28]{0:T(128)}, u32[]{:S(2)}) copy-start(f32[28]{0:T(128)} %param.29) | copy-start | bytes 340
  532.1 790.8 %all-gather.5.cloned.1.call-start = ((), (), s32[]{:S(2)}) async-start(), calls=%async_computation | async-start | bytes 2113536 | tf_op jit(solution)/shard_map/all_gather | solution.py:64
  810.2 787.7 %all-reduce.8.cloned.1.call-start = ((), (), s32[]{:S(2)}) async-start(), calls=%async_computation.2 | async-start | bytes 524288 | tf_op jit(solution)/shard_map/psum | solution.py:58
  1326.4 359.6 %all-gather.7.cloned.1.call-start = ((), (), s32[]{:S(2)}) async-start(), calls=%async_computation.1 | async-start | bytes 2113536 | tf_op jit(solution)/shard_map/all_gather | solution.py:64
  1607.1 4.1 copy-start.4
  1607.1 4.1 copy-start.5
  1687.9 2.0 copy-start.6
  1687.9 2.0 copy-start.7
Sparse Core Ops, SparseCore 0:
  532.2 267.5 all-reduce.9
  810.3 77.6 all-gather.4
  1326.5 271.3 all-reduce.7
  1608.4 77.5 all-gather.6
